TPU v7x, 32 devices: a whole 2x2x4 slice. The times are simulated.
32 devices in a mesh: row: 8 (over y, x, core), col: 4 (over z).
Axes of the slice: x: 2, y: 2, z: 4, core: 2. Of those that a mesh axis runs over, the one named last changes fastest.
Arguments:
- matrix: float32 [16, 8, 128, 32, 4, 128], P(None, 'row', None, None, 'col'), may hold values from -6 to 6
- reflectors: float32 [32, 4, 128, 512], P(None, 'col'), as said below
Outputs:
- updated: float32 [16, 8, 128, 32, 4, 128], P(None, 'row', None, None, 'col')
Inputs may be any that keep to these rules, and one draw needn't show every extreme that they name: Read as a 16384 x 512 matrix, the columns of reflectors are orthonormal.
All inputs are finite; a program needn't handle non-finite values.
Results may differ from a plain program's by a relative error of at most 0.0001.
Values sent between devices are 32-bit elements; how exact they have to be, the bound alone decides.
No kernel may reach another device: no remote copies, remote signals or barrier semaphores. Data moves between devices by JAX's collectives and lax.ppermute only.
A program may use at most 192 MiB of HBM per device.

v0:
```python
import jax
import jax.numpy as jnp
from jax import lax
from jax.sharding import PartitionSpec as P


def from_root(value, axis, source):
    kept = jnp.where(lax.axis_index(axis) == source, value, 0).astype(value.dtype)
    return lax.psum(kept, axis)


def per_device(matrix, reflectors):
    row_count = lax.axis_size("row")
    col_count = lax.axis_size("col")
    stride = row_count // col_count
    row_index = lax.axis_index("row")
    col_index = lax.axis_index("col")
    row_tiles, _, tile_size, col_tiles, _, _ = matrix.shape
    total_rank = reflectors.shape[3]
    local_rows = row_tiles * tile_size
    local_cols = col_tiles * tile_size
    current = matrix.reshape(local_rows, local_cols)
    row_ids = (
        (jnp.arange(row_tiles)[:, None] * row_count + row_index) * tile_size
        + jnp.arange(tile_size)[None, :]
    ).reshape(-1)
    col_ids = (
        (jnp.arange(col_tiles)[:, None] * col_count + col_index) * tile_size
        + jnp.arange(tile_size)[None, :]
    ).reshape(-1)
    lower_mask = row_ids[:, None] >= col_ids[None, :]
    strict_mask = row_ids[:, None] > col_ids[None, :]
    refl_cols = reflectors.reshape(local_cols, total_rank)

    def pick_rows(source):
        breadth = source.shape[1]
        blocks = source.reshape(row_tiles, stride, tile_size, breadth)
        chosen = lax.dynamic_index_in_dim(blocks, row_index // col_count, axis=1, keepdims=False)
        return chosen.reshape(local_rows, breadth)

    def matmul(left_side, right_side):
        return jnp.dot(
            left_side,
            right_side,
            precision=lax.Precision.HIGHEST,
            preferred_element_type=jnp.float32,
        )

    def inner(left_side, right_side):
        return lax.dot_general(
            left_side,
            right_side,
            (((0,), (0,)), ((), ())),
            precision=lax.Precision.HIGHEST,
            preferred_element_type=jnp.float32,
        )

    refl_rows = from_root(pick_rows(refl_cols), "col", row_index % col_count)
    direct_part = matmul(jnp.where(lower_mask, current, 0.0), refl_cols)
    trans_part = inner(jnp.where(strict_mask, current, 0.0), refl_rows)
    direct = lax.psum(direct_part, "col")
    transposed = lax.psum(trans_part, "row")
    w_rows = direct + from_root(pick_rows(transposed), "col", row_index % col_count)
    breadth = direct.shape[1]
    pieces = []
    for offset in range(stride):
        moved = from_root(direct, "row", col_index + offset * col_count)
        pieces.append(moved.reshape(row_tiles, tile_size, breadth))
    w_cols = transposed + jnp.stack(pieces, axis=1).reshape(local_cols, breadth)
    projection = lax.psum(inner(refl_rows, w_rows), "row")
    w_rows = w_rows - 0.5 * matmul(refl_rows, projection)
    w_cols = w_cols - 0.5 * matmul(refl_cols, projection)
    left_side = jnp.concatenate([refl_rows, w_rows], axis=1)
    right_side = jnp.concatenate([w_cols, refl_cols], axis=1)
    current = current - lax.dot_general(
        left_side,
        right_side,
        (((1,), (1,)), ((), ())),
        precision=lax.Precision.HIGHEST,
        preferred_element_type=jnp.float32,
    )
    return jnp.where(lower_mask, current, 0.0).reshape(matrix.shape)


def solution(mesh):
    placed = (P(None, "row", None, None, "col", None), P(None, "col", None, None))
    return jax.shard_map(
        per_device,
        mesh=mesh,
        in_specs=placed,
        out_specs=P(None, "row", None, None, "col", None),
        check_vma=False,
    )
```

profile of v0, /device:TPU:0, one launch (start us, length us, event | category | flops | bytes accessed | tf_op | source)
XLA Modules:
  0.0 1057.2 jit_solution(7333891088313638128)
XLA Ops:
  6.5 4.9 bitcast_select_fusion.3
  11.4 0.0 all-reduce.9.cloned.1.call-start
  11.5 0.1 iota_add_fusion.1
  11.6 0.1 iota_add_fusion
  11.7 157.6 %all-reduce.7.cloned.1.call-done = f32[2048,512]{1,0:T(8,128)} async-done(((f32[2048,512]{1,0:T(8,128)}), f32[2048,512]{1,0:T(8,128)}) %all-reduce.7.cloned.1.call-update) | async-done | bytes 4194320 | tf_op jit(solution)/shard_map/psum | solution.py:9
  169.3 67.3 %fusion.4 = f32[4096,512]{1,0:T(8,128)} fusion(f32[2048,512]{1,0:T(8,128)} %all-reduce.7.cloned.1.call-done, f32[256,8,32,128]{3,2,1,0:T(8,128)} %bitcast.60, s32[4096]{0:T(1024)S(1)} %get-tuple-element.16, s32[2048]{0:T(1024)S(1)} %get-tuple-element.14), kind=kOutput, calls=%fused_computation.7 | convolution fusion | flops 51556384768 | bytes 46161920 | tf_op jit(solution)/shard_map/dot_general | solution.py:50
  236.6 0.0 all-reduce.13.cloned.1.call-start
  236.7 114.5 %fusion = f32[16,128,32,128]{3,2,1,0:T(8,128)} fusion(f32[16,1,128,32,1,128]{5,4,3,2,1,0:T(1,128)} %param.2, s32[32,128]{1,0:T(8,128)S(1)} %get-tuple-element.15, s32[16,128]{1,0:T(8,128)S(1)} %get-tuple-element.13), kind=kLoop, calls=%fused_computation.1 | loop fusion | flops 16777216 | bytes 67133440 | tf_op jit(solution)/shard_map/jit(_where)/select_n | solution.py:59
  351.1 64.4 %fusion.1 = f32[2048,512]{1,0:T(8,128)} fusion(f32[4096,512]{1,0:T(8,128)} %bitcast.64, f32[256,8,32,128]{3,2,1,0:T(8,128)} %bitcast.62), kind=kOutput, calls=%fused_computation.2 | convolution fusion | flops 51539607552 | bytes 46137344 | tf_op jit(solution)/shard_map/dot_general | solution.py:42
  415.5 4.9 bitcast_select_fusion.2
  420.4 0.0 all-reduce.11.cloned.1.call-start
  420.5 289.9 %all-reduce.13.cloned.1.call-done = (f32[2048,512]{1,0:T(8,128)}, f32[2048,512]{1,0:T(8,128)}) async-done(((f32[2048,512]{1,0:T(8,128)}, f32[2048,512]{1,0:T(8,128)}), (f32[2048,512]{1,0:T(8,128)}, f32[2048,512]{1,0:T(8,128)})) %all-reduce.13.cloned.1.call-update) | async-done | bytes 8388624 | tf_op jit(solution)/shard_map/psum | solution.py:61
  710.4 9.0 fusion.22
  719.4 2.0 copy-done
  721.4 7.7 fusion.23
  729.1 136.8 %all-reduce.11.cloned.1.call-done = (f32[16,1,128,512]{3,2,0,1:T(8,128)}, f32[16,1,128,512]{3,2,0,1:T(8,128)}, f32[512,512]{1,0:T(8,128)}) async-done(((f32[16,1,128,512]{3,2,0,1:T(8,128)}, f32[16,1,128,512]{3,2,0,1:T(8,128)}, f32[512,512]{1,0:T(8,128)}), (f32[16,1,128,512]{3,2,0,1:T(8,128)}, f32[16,1,128,512]{3,2,0,1:T(8,128)}, f32[512,512]{1,0:T(8,128)})) %all-reduce.11.cloned.1.call-update) | async-done | bytes 9437200 | tf_op jit(solution)/shard_map/psum | solution.py:9
  865.9 4.5 pad_maximum_fusion
  870.4 1.6 copy.5
  872.0 0.6 copy-done.1
  872.6 0.3 copy-done.3
  872.9 10.3 multiply_subtract_fusion
  883.2 18.6 %bitcast_subtract_fusion.1 = f32[4096,512]{1,0:T(8,128)} fusion(f32[4096,512]{1,0:T(8,128)} %all-reduce.9.cloned.1.call-done, f32[16,2,128,512]{3,2,1,0:T(8,128)S(1)} %copy.5, f32[512,512]{1,0:T(8,128)S(1)} %copy-done.3, f32[4096,512]{1,0:T(8,128)} %bitcast.65), kind=kOutput, calls=%fused_computation.22 | convolution fusion | flops 12891193344 | bytes 34603008 | tf_op jit(solution)/shard_map/dot_general | solution.py:42
  901.8 121.1 %fusion.6 = f32[256,8,32,128]{3,1,2,0:T(8,128)} fusion(f32[256,8,32,128]{3,2,1,0:T(8,128)} %bitcast.61, f32[4096,512]{1,0:T(8,128)} %bitcast.66, f32[4096,512]{1,0:T(8,128)} %bitcast_subtract_fusion.1, s32[4096]{0:T(1024)S(1)} %get-tuple-element.16, s32[2048]{0:T(1024)S(1)} %get-tuple-element.14, f32[2048,512]{1,0:T(8,128)} %multiply_subtract_fusion, ...), kind=kOutput, calls=%fused_computation.9 | convolution fusion | flops 103110672384 | bytes 92299264 | tf_op jit(solution)/shard_map/dot_general | solution.py:75
  1022.9 27.6 %copy.11 = f32[256,8,32,128]{3,2,1,0:T(8,128)} copy(f32[256,8,32,128]{3,1,2,0:T(8,128)} %fusion.6) | data formatting | bytes 67108864
  (13 shorter events, 0.1 us)
Async XLA Ops:
  6.5 162.8 %all-reduce.7.cloned.1.call-start = ((), (), s32[]{:S(2)}) async-start(), calls=%async_computation | async-start | bytes 8388608 | tf_op jit(solution)/shard_map/psum | solution.py:9
  11.4 404.1 %all-reduce.9.cloned.1.call-start = ((), (), s32[]{:S(2)}) async-start(), calls=%async_computation.1 | async-start | bytes 16777216 | tf_op jit(solution)/shard_map/psum | solution.py:62
  236.6 473.8 %all-reduce.13.cloned.1.call-start = ((), (), s32[]{:S(2)}) async-start(), calls=%async_computation.3 | async-start | bytes 16777216 | tf_op jit(solution)/shard_map/psum | solution.py:61
  420.4 445.5 %all-reduce.11.cloned.1.call-start = ((), (), s32[]{:S(2)}) async-start(), calls=%async_computation.2 | async-start | bytes 18874368 | tf_op jit(solution)/shard_map/psum | solution.py:9
  710.4 11.0 %copy-start.2 = (f32[2048,512]{1,0:T(8,128)S(1)}, f32[2048,512]{1,0:T(8,128)}, u32[]{:S(2)}) copy-start(f32[2048,512]{1,0:T(8,128)} %all-reduce.7.cloned.1.call-done) | copy-start | bytes 12582916
  719.4 2.0 copy-start
  870.4 2.2 copy-start.1
  870.4 2.5 copy-start.3
Sparse Core Ops, SparseCore 0:
  11.6 157.6 all-reduce.6
  236.7 125.1 all-reduce.8
  420.6 289.8 all-reduce.12
  729.3 136.6 all-reduce.10
where the time goes:
time: 1070 us; the launch traced here: 1060 us
  waiting for transfers between devices  584 us (55%)
  matrix products  289 us (27%)
  other arithmetic  138 us (13%)
  local copies, waits for them, and re-layouts  32 us (3%)
  between operations  13.4 us (1%)
    psum x2, waiting for transfers between devices, from_root(): return lax.psum(kept, axis)  294 us
    psum x1, waiting for transfers between devices, per_device(): direct = lax.psum(direct_part, 'col')  290 us
    dot_general x1, matrix products, per_device(): lax.dot_general(left_side, right_side, (((1,), (1,)), ((), ())), precisio...  121 us
    select_n x1, other arithmetic, per_device(): direct_part = matmul(jnp.where(lower_mask, current, 0.0), refl_cols)  114 us
    dot_general x3, matrix products, matmul(): jnp.dot(left_side, right_side, precision=lax.Precision.HIGHEST, preferred...  93.3 us
    dot_general x2, matrix products, inner(): lax.dot_general(left_side, right_side, (((0,), (0,)), ((), ())), precisio...  75 us
    unnamed x9, local copies, waits for them, and re-layouts  30.4 us
  transfers between devices with their start and end apart: 4, of which 3 were waited for; matrix products, arithmetic and copies ran while one was open for 17% of the time, Pallas kernels for 0%

commit v1 on v0

v1 whole, which is shorter than its diff:
```python
import functools

import jax
import jax.numpy as jnp
import numpy as np
from jax import lax
from jax.experimental import pallas as pl
from jax.experimental.pallas import tpu as pltpu
from jax.sharding import PartitionSpec as P

F32 = jnp.float32
BF16 = jnp.bfloat16
BLOCK_TILES = 4
PANELS = 2


def split(x):
    high = x.astype(BF16)
    return high, (x - high.astype(F32)).astype(BF16)


def dot1(a, b, ca, cb):
    return lax.dot_general(a, b, (((ca,), (cb,)), ((), ())), preferred_element_type=F32)


def dot3(a, b, ca, cb):
    return dot1(a[0], b[0], ca, cb) + dot1(a[0], b[1], ca, cb) + dot1(a[1], b[0], ca, cb)


class Plan:
    def __init__(self, row_tiles, tile, col_tiles, row_count, col_count):
        self.tile, self.row_tiles, self.col_tiles = tile, row_tiles, col_tiles
        self.row_count, self.col_count = row_count, col_count
        self.stride = row_count // col_count
        self.br = BLOCK_TILES
        self.bc = BLOCK_TILES * self.stride
        self.blocks = row_tiles // self.br
        self.rows, self.cols = self.br * tile, self.bc * tile

    def ids(self, shape, a, b, place):
        r = lax.broadcasted_iota(jnp.int32, shape, 0) + a * self.rows
        c = lax.broadcasted_iota(jnp.int32, shape, 1) + b * self.cols
        t = self.tile
        gr = ((r // t) * self.row_count + place[0]) * t + r % t
        gc = ((c // t) * self.col_count + place[1]) * t + c % t
        return gr, gc

    def load(self, ref):
        return jnp.concatenate([ref[:, m, :] for m in range(self.bc)], axis=1)

    def half_lower(self, ref, a, b, place):
        x = self.load(ref)
        gr, gc = self.ids(x.shape, a, b, place)
        return jnp.where(gr > gc, x, jnp.where(gr == gc, 0.5 * x, 0.0))

    def tables(self, pairs):
        return tuple(jnp.asarray(np.array([p[n] for p in pairs], np.int32)) for n in (0, 1))

    def a_spec(self, index):
        return pl.BlockSpec((self.rows, self.bc, self.tile), index)

    def params(self):
        return pltpu.CompilerParams(vmem_limit_bytes=60 << 20)


def first_kernel(plan, at, bt, place, a_ref, v_ref, o0_ref, o1_ref, h_ref, l_ref, vh, vl):
    g = pl.program_id(0)
    a, b = at[g], bt[g]

    @pl.when(g == 0)
    def _():
        vh[...], vl[...] = split(v_ref[...])

    x = split(plan.half_lower(a_ref, a, b, place))
    h_ref[...], l_ref[...] = x
    s = pl.ds(pl.multiple_of(b * plan.cols, plan.cols), plan.cols)
    d = dot3(x, (vh[s, :], vl[s, :]), 1, 0)
    w = o0_ref.shape[1]

    @pl.when(b == 0)
    def _():
        o0_ref[...] = d[:, :w]
        o1_ref[...] = d[:, w:]

    @pl.when(b > 0)
    def _():
        o0_ref[...] += d[:, :w]
        o1_ref[...] += d[:, w:]


def whole(x):
    return pl.BlockSpec(x.shape, lambda g, *_: (0, 0), pipeline_mode=pl.Buffered(1))


def cost(plan, n, passes=3):
    area = plan.rows * plan.cols * (plan.blocks * (plan.blocks + 1) // 2)
    return pl.CostEstimate(flops=2 * passes * area * n, bytes_accessed=4 * area, transcendentals=0)


def direct_first(plan, a, v, place):
    at, bt = plan.tables([(i, j) for i in range(plan.blocks) for j in range(i + 1)])
    n = v.shape[1]
    block = pl.BlockSpec((plan.rows, plan.cols), lambda g, at, bt, p: (at[g], bt[g]))
    flat = jax.ShapeDtypeStruct((a.shape[0], a.shape[1] * a.shape[2]), BF16)
    return pl.pallas_call(
        functools.partial(first_kernel, plan),
        grid_spec=pltpu.PrefetchScalarGridSpec(
            num_scalar_prefetch=3,
            grid=(at.shape[0],),
            in_specs=[plan.a_spec(lambda g, at, bt, p: (at[g], bt[g], 0)), whole(v)],
            out_specs=[pl.BlockSpec((plan.rows, n // 2), lambda g, at, bt, p: (at[g], 0))] * 2 + [block, block],
            scratch_shapes=[pltpu.VMEM(v.shape, BF16)] * 2,
        ),
        out_shape=[jax.ShapeDtypeStruct((a.shape[0], n // 2), F32)] * 2 + [flat, flat],
        cost_estimate=cost(plan, n),
        compiler_params=plan.params(),
        name="direct_first",
    )(at, bt, place, a, v)


def trans_kernel(plan, at, bt, h_ref, l_ref, v_ref, o_ref, vh, vl):
    g = pl.program_id(0)
    a, b = at[g], bt[g]

    @pl.when(g == 0)
    def _():
        vh[...], vl[...] = split(v_ref[...])

    s = pl.ds(pl.multiple_of(a * plan.rows, plan.rows), plan.rows)
    d = dot3((h_ref[...], l_ref[...]), (vh[s, :], vl[s, :]), 0, 0)

    @pl.when(a == b)
    def _():
        o_ref[...] = d

    @pl.when(a > b)
    def _():
        o_ref[...] += d


def trans(plan, h, l, v):
    at, bt = plan.tables([(i, j) for j in range(plan.blocks) for i in range(j, plan.blocks)])
    n = v.shape[1]
    block = pl.BlockSpec((plan.rows, plan.cols), lambda g, at, bt: (at[g], bt[g]))
    return pl.pallas_call(
        functools.partial(trans_kernel, plan),
        grid_spec=pltpu.PrefetchScalarGridSpec(
            num_scalar_prefetch=2,
            grid=(at.shape[0],),
            in_specs=[block, block, whole(v)],
            out_specs=pl.BlockSpec((plan.cols, n), lambda g, at, bt: (bt[g], 0)),
            scratch_shapes=[pltpu.VMEM(v.shape, BF16)] * 2,
        ),
        out_shape=jax.ShapeDtypeStruct((h.shape[1], n), F32),
        cost_estimate=cost(plan, n),
        compiler_params=plan.params(),
        name="trans",
    )(at, bt, h, l, v)


def near_kernel(plan, panels, at, bt, *refs):
    a_ref, vr = refs[0], refs[1 : 1 + panels]
    yc = refs[1 + panels : 1 + 2 * panels]
    o_ref, vrh, vrl, ych, ycl = refs[1 + 2 * panels :]
    g = pl.program_id(0)
    a, b = at[g], bt[g]
    w = ych.shape[1] // panels

    @pl.when(g == 0)
    def _():
        for p in range(panels):
            vrh[:, p * w : (p + 1) * w], vrl[:, p * w : (p + 1) * w] = split(vr[p][...])

    @pl.when(a == b)
    def _():
        for p in range(panels):
            ych[:, p * w : (p + 1) * w], ycl[:, p * w : (p + 1) * w] = split(yc[p][...])

    s = pl.ds(pl.multiple_of(a * plan.rows, plan.rows), plan.rows)
    o_ref[...] = plan.load(a_ref) - dot3((vrh[s, :], vrl[s, :]), (ych[...], ycl[...]), 1, 1)


def near(plan, a, vr, yc):
    at, bt = plan.tables([(i, j) for j in range(plan.blocks) for i in range(j, plan.blocks)])
    w = vr[0].shape[1]
    n = w * len(vr)
    strip = lambda q: pl.BlockSpec((plan.cols, w), lambda g, at, bt: (bt[g], q))
    return pl.pallas_call(
        functools.partial(near_kernel, plan, len(yc)),
        grid_spec=pltpu.PrefetchScalarGridSpec(
            num_scalar_prefetch=2,
            grid=(at.shape[0],),
            in_specs=[plan.a_spec(lambda g, at, bt: (at[g], bt[g], 0))] + [whole(v) for v in vr] + [strip(q) for _, q in yc],
            out_specs=pl.BlockSpec((plan.rows, plan.cols), lambda g, at, bt: (at[g], bt[g])),
            scratch_shapes=[pltpu.VMEM((a.shape[0], n), BF16)] * 2 + [pltpu.VMEM((plan.cols, n), BF16)] * 2,
        ),
        out_shape=jax.ShapeDtypeStruct((a.shape[0], a.shape[1] * a.shape[2]), F32),
        cost_estimate=cost(plan, n),
        compiler_params=plan.params(),
        name="near",
    )(at, bt, a, *vr, *[y for y, _ in yc])


def far_kernel(plan, at, bt, place, x_ref, y_ref, v_ref, o_ref, yh, yl, vh, vl):
    g = pl.program_id(0)
    a, b = at[g], bt[g]

    @pl.when(g == 0)
    def _():
        yh[...], yl[...] = split(y_ref[...])

    @pl.when(a == b)
    def _():
        vh[...], vl[...] = split(v_ref[...])

    @pl.when(b > a)
    def _():
        o_ref[...] = jnp.zeros(o_ref.shape, F32)

    @pl.when(b <= a)
    def _():
        s = pl.ds(pl.multiple_of(a * plan.rows, plan.rows), plan.rows)
        x = x_ref[...] - dot3((yh[s, :], yl[s, :]), (vh[...], vl[...]), 1, 1)
        gr, gc = plan.ids(x.shape, a, b, place)
        x = jnp.where(gr >= gc, x, 0.0)
        for m in range(plan.bc):
            o_ref[:, m, :] = x[:, m * plan.tile : (m + 1) * plan.tile]


def far(plan, x, y, v, q, place):
    at, bt = plan.tables([(i, j) for j in range(plan.blocks) for i in range(plan.blocks)])
    n = y.shape[1]
    return pl.pallas_call(
        functools.partial(far_kernel, plan),
        grid_spec=pltpu.PrefetchScalarGridSpec(
            num_scalar_prefetch=3,
            grid=(at.shape[0],),
            in_specs=[
                pl.BlockSpec((plan.rows, plan.cols), lambda g, at, bt, p: (jnp.maximum(at[g], bt[g]), bt[g])),
                whole(y),
                pl.BlockSpec((plan.cols, n), lambda g, at, bt, p: (bt[g], q)),
            ],
            out_specs=plan.a_spec(lambda g, at, bt, p: (at[g], bt[g], 0)),
            scratch_shapes=[pltpu.VMEM(y.shape, BF16)] * 2 + [pltpu.VMEM((plan.cols, n), BF16)] * 2,
        ),
        out_shape=jax.ShapeDtypeStruct((x.shape[0], x.shape[1] // plan.tile, plan.tile), F32),
        cost_estimate=cost(plan, n),
        compiler_params=plan.params(),
        name="far",
    )(at, bt, place, x, y, v)


def high(a, b, ca, cb):
    return lax.dot_general(
        a, b, (((ca,), (cb,)), ((), ())), precision=lax.Precision.HIGH, preferred_element_type=F32
    )


def body(matrix, reflectors):
    row_count, col_count = lax.axis_size("row"), lax.axis_size("col")
    row, col = lax.axis_index("row"), lax.axis_index("col")
    row_tiles, _, tile, col_tiles, _, _ = matrix.shape
    rank = reflectors.shape[3]
    plan = Plan(row_tiles, tile, col_tiles, row_count, col_count)
    stride = plan.stride
    rows, cols = row_tiles * tile, col_tiles * tile
    a = matrix.reshape(rows, col_tiles, tile)
    place = jnp.stack([row, col]).astype(jnp.int32)
    both = ("row", "col")
    part = row // col_count
    gap = jnp.bitwise_xor(row % col_count, col)
    bits = [1 << n for n in range(col_count.bit_length() - 1)]
    vc = reflectors.reshape(cols, rank)
    width = rank // PANELS

    def own_rows(x):
        blocks = x.reshape(row_tiles, stride, tile, x.shape[1])
        return lax.dynamic_index_in_dim(blocks, part, axis=1, keepdims=False).reshape(rows, x.shape[1])

    def pairs(keep, bit):
        out = []
        for i in range(row_count):
            for z in range(col_count):
                if keep((i % col_count) ^ z):
                    out.append((i * col_count + z, i * col_count + (z ^ bit)))
        return out

    def tie(x, *after):
        return lax.optimization_barrier((x, *after))[0]

    def hop_out(x, bit):
        done = sum(n for n in bits if n > bit)
        return lax.ppermute(x, both, pairs(lambda code: code & ~done == 0, bit))

    def take(x, got, bit):
        mine = (jnp.bitwise_and(gap, bit) != 0) & (jnp.bitwise_and(gap, bit - 1) == 0)
        return jnp.where(mine, got, x)

    def mid_out(x):
        for bit in reversed(bits[1:-1]):
            x = take(x, hop_out(x, bit), bit)
        return x

    def mid_in(x):
        for bit in bits[1:-1]:
            x = x + hop_in(x, bit)
        return x

    def hop_in(x, bit):
        return lax.ppermute(x, both, pairs(lambda code: code & bit and code & (bit - 1) == 0, bit))

    def swap(x, axis, count, bit):
        return lax.ppermute(x, axis, [(n, n ^ bit) for n in range(count)])

    def halves(x, bit):
        x = x.reshape(2, x.shape[0] // 2, *x.shape[1:])
        mine = (jnp.bitwise_and(row, bit) != 0).astype(jnp.int32)
        keep = lax.dynamic_index_in_dim(x, mine, 0, keepdims=False)
        send = lax.dynamic_index_in_dim(x, 1 - mine, 0, keepdims=False)
        return keep, send

    def joined(x, got, bit):
        upper = jnp.bitwise_and(row, bit) != 0
        return jnp.concatenate([jnp.where(upper, got, x), jnp.where(upper, x, got)], axis=0)

    def collect(x, order):
        for bit in reversed(order):
            x = joined(x, swap(x, "row", row_count, bit), bit)
        return x

    row_bits = [1 << n for n in range(row_count.bit_length() - 1)]
    others = row_count // 2
    chip = row // 2

    def cross(x, code):
        return lax.ppermute(x, "row", [(n, n ^ (2 * code)) for n in range(row_count)])

    def sum_steps(x):
        keep, send = halves(x, 1)
        got = swap(send, "row", row_count, 1)
        prev = yield
        x = tie(keep, prev) + got
        x = x.reshape(others, x.shape[0] // others, x.shape[1])
        pick = lambda code: lax.dynamic_index_in_dim(x, jnp.bitwise_xor(chip, code), 0, keepdims=False)
        got = [cross(pick(code), code) for code in range(1, others)]
        prev = yield x
        piece = tie(pick(0), prev)
        for g in got:
            piece = piece + g
        got = [cross(piece, code) for code in range(1, others)]
        prev = yield piece
        stack = [tie(piece, prev)] + got
        bit = 1
        while bit < others:
            flip = jnp.bitwise_and(chip, bit) != 0
            stack = [jnp.where(flip, stack[n ^ bit], stack[n]) for n in range(others)]
            bit *= 2
        x = jnp.concatenate(stack, axis=0)
        got = swap(x, "row", row_count, 1)
        prev = yield x
        yield joined(tie(x, prev), got, 1)

    own = own_rows(vc)
    own = lax.optimization_barrier([own[:, p * width : (p + 1) * width] for p in range(PANELS)])

    def with_direct(t, dp):
        t = t.reshape(row_tiles, stride, tile, width)
        here = (jnp.arange(stride) == part)[None, :, None, None] & (gap == 0)
        t = t + jnp.where(here, dp.reshape(row_tiles, 1, tile, width), 0.0)
        return t.reshape(cols, width)

    ga0 = hop_out(own[0], bits[-1])
    d0, d1, high_part, low_part = direct_first(plan, a, vc, place)
    b0 = hop_in(d0, bits[0])
    x0 = mid_out(take(own[0], tie(ga0, d1), bits[-1]))
    gb0 = hop_out(x0, bits[0])
    d0 = mid_in(tie(d0, x0) + b0)
    a0 = hop_in(d0, bits[-1])
    ga1 = hop_out(tie(own[1], d0), bits[-1])
    v0 = take(tie(x0, d0), gb0, bits[0])
    t0 = trans(plan, high_part, low_part, v0)
    t0 = with_direct(t0, tie(d0, t0) + a0)
    s0 = sum_steps(t0)
    next(s0)
    x1 = mid_out(take(tie(own[1], t0), ga1, bits[-1]))
    gb1 = hop_out(x1, bits[0])
    b1 = hop_in(tie(d1, x1), bits[0])
    e = s0.send(x1)
    d1 = mid_in(tie(d1, e) + b1)
    a1 = hop_in(d1, bits[-1])
    v1 = take(tie(x1, d1), gb1, bits[0])
    t1 = trans(plan, high_part, low_part, v1)
    e = s0.send(t1)
    e = s0.send(e)
    d1 = tie(d1, e) + a1
    s1 = sum_steps(with_direct(t1, d1))
    next(s1)
    e = d1
    y0 = s0.send(e)
    e = s1.send(y0)
    oy0 = own_rows(y0)
    ga0 = hop_out(oy0, bits[-1])
    e = s1.send(oy0)
    x0 = mid_out(take(tie(oy0, e), ga0, bits[-1]))
    gb0 = hop_out(x0, bits[0])
    e = s1.send(x0)
    y1 = s1.send(e)
    oy1 = own_rows(y1)
    ga1 = hop_out(oy1, bits[-1])
    piece = rank // row_count
    mine = lax.dynamic_slice_in_dim(vc, row * piece, piece, axis=1)
    m = [high(tie(mine, oy1), y, 0, 0) for y in (y0, y1)]
    m = jnp.concatenate(m, axis=1)
    got = swap(m, "col", col_count, bits[-1])
    x = near(plan, a, [v0, v1], [(tie(y0, m), 0), (y1, 0)])
    m = tie(m, x) + got
    for bit in reversed(bits[:-1]):
        m = m + swap(m, "col", col_count, bit)
    x1 = mid_out(take(tie(oy1, m), ga1, bits[-1]))
    gb1 = hop_out(x1, bits[0])
    m = collect(tie(m, x1), row_bits[::-1])
    fix = high(jnp.concatenate([v0, v1], axis=1), m, 1, 0)
    r0 = take(tie(x0, fix), gb0, bits[0])
    r1 = take(tie(x1, r0), gb1, bits[0])
    yr = jnp.concatenate([r0, r1], axis=1) - fix
    return far(plan, x, yr, vc, 0, place).reshape(matrix.shape)


def solution(mesh):
    placed = (P(None, "row", None, None, "col", None), P(None, "col", None, None))
    return jax.shard_map(
        body,
        mesh=mesh,
        in_specs=placed,
        out_specs=P(None, "row", None, None, "col", None),
        check_vma=False,
    )
```

time: 1070 us -> 526 us (0.49)
  waiting for transfers between devices: 584 us -> 212 us
  matrix products: 289 us -> 7.51 us
  Pallas kernels: 0 us -> 156 us
  other arithmetic: 138 us -> 43.5 us
  starting transfers between devices: 0.13 us -> 80.2 us
  between operations: 13.4 us -> 0.49 us
    psum x4 -> x0, waiting for transfers between devices: 584 us -> none  [the longest x2 294 us: from_root(): return lax.psum(kept, axis)]
    dot_general x6 -> x3, matrix products: 289 us -> 7.51 us  [high(): lax.dot_general(a, b, (((ca,), (cb,)), ((), ())), precision=lax.Precision...]
    ppermute x0 -> x33, waiting for transfers between devices: none -> 212 us  [the longest x4 118 us: hop_in(): lax.ppermute(x, both, pairs(lambda code: code & bit and code & bit - 1 ==...]
    pallas_call x0 -> x5, Pallas kernels: none -> 156 us  [the longest x1 44.2 us: far(): pl.pallas_call(functools.partial(far_kernel, plan), grid_spec=pltpu.Prefe...]
    select_n x3 -> x15, other arithmetic: 124 us -> 21.5 us  [the longest x8 17 us: take(): return jnp.where(mine, got, x)]
    ppermute x0 -> x33, starting transfers between devices: none -> 80.2 us  [the longest x8 43.1 us: hop_out(): return lax.ppermute(x, both, pairs(lambda code: code & ~done == 0, bit))]
    unnamed x9 -> x24, local copies, waits for them, and re-layouts: 30.4 us -> 8.62 us
  transfers between devices with their start and end apart: 4 -> 33, of which waited for: 3 -> 17; matrix products, arithmetic and copies ran while one was open for 17% -> 8% of each run, Pallas kernels for 0% -> 21%
where the time goes in v1:
time: 526 us; the launch traced here: 522 us
  waiting for transfers between devices  212 us (40%)
  Pallas kernels  156 us (30%)
  starting transfers between devices  80.2 us (15%)
  other arithmetic  43.5 us (8%)
  local copies, waits for them, and re-layouts  21.8 us (4%)
  matrix products  7.51 us (1%)
    ppermute x4, waiting for transfers between devices, hop_in(): lax.ppermute(x, both, pairs(lambda code: code & bit and code & bit - 1 ==...  118 us
    ppermute x12, waiting for transfers between devices, cross(): return lax.ppermute(x, 'row', [(n, n ^ 2 * code) for n in range(row_count)])  57 us
    pallas_call x1, Pallas kernels, far(): pl.pallas_call(functools.partial(far_kernel, plan), grid_spec=pltpu.Prefe...  44.2 us
    ppermute x8, starting transfers between devices, hop_out(): return lax.ppermute(x, both, pairs(lambda code: code & ~done == 0, bit))  43.1 us
    pallas_call x1, Pallas kernels, direct_first(): pl.pallas_call(functools.partial(first_kernel, plan), grid_spec=pltpu.Pre...  41.8 us
    pallas_call x2, Pallas kernels, trans(): pl.pallas_call(functools.partial(trans_kernel, plan), grid_spec=pltpu.Pre...  36.2 us
    pallas_call x1, Pallas kernels, near(): pl.pallas_call(functools.partial(near_kernel, plan, len(yc)), grid_spec=p...  34 us
    ppermute x9, waiting for transfers between devices, swap(): return lax.ppermute(x, axis, [(n, n ^ bit) for n in range(count)])  19.1 us
  transfers between devices with their start and end apart: 33, of which 17 were waited for; matrix products, arithmetic and copies ran while one was open for 8% of the time, Pallas kernels for 21%

profile of v1, /device:TPU:0, one launch (start us, length us, event | category | flops | bytes accessed | tf_op | source)
XLA Modules:
  0.0 521.5 jit_solution(240820783424510494)
XLA Ops:
  4.6 7.3 %collective-permute-start = (f32[2048,256]{1,0:T(8,128)S(1)}, f32[2048,256]{1,0:T(8,128)}, u32[]{:S(2)}, u32[]{:S(2)}) collective-permute-start(f32[2048,256]{1,0:T(8,128)S(1)} %get-tuple-element.36), channel_id=1, source_target_pairs={{0,2},{5,7},{10,8},{15,13},{16,18},{21,23},{26,24},{31,29}} | collective-permute-start | bytes 6291464 | tf_op jit(solution)/shard_map/ppermute | solution.py:293
  12.5 41.8 %direct_first.1 = (f32[2048,256]{1,0:T(8,128)}, f32[2048,256]{1,0:T(8,128)}, bf16[2048,4096]{1,0:T(8,128)(2,1)}, bf16[2048,4096]{1,0:T(8,128)(2,1)}) custom-call(s32[10]{0:T(128)} %constant.104.clone.at, s32[10]{0:T(128)} %constant.105.clone.bt, s32[2]{0:T(128)} %pad_add_fusion.place, f32[2048,32,128]{2,1,0:T(8,128)} %bitcast.53, f32[4096,512]{1,0:T(8,128)} %bitcast.58), custom_call_target="tpu_custom_call" | custom-call | flops 16106127360 | bytes 20971520 | tf_op jit(solution)/shard_map/direct_first/pallas_call | solution.py:105
  57.7 7.3 %collective-permute-start.1 = (f32[2048,256]{1,0:T(8,128)S(1)}, f32[2048,256]{1,0:T(8,128)}, u32[]{:S(2)}, u32[]{:S(2)}) collective-permute-start(f32[2048,256]{1,0:T(8,128)S(1)} %broadcast_select_fusion.7), channel_id=1, source_target_pairs={{0,1},{2,3},{5,4},{7,6},{8,9},{10,11},{13,12},{15,14},{16,17},{18,... | collective-permute-start | bytes 6291464 | tf_op jit(solution)/shard_map/ppermute | solution.py:293
  65.0 35.1 %collective-permute-done.2 = f32[2048,256]{1,0:T(8,128)} collective-permute-done((f32[2048,256]{1,0:T(8,128)}, f32[2048,256]{1,0:T(8,128)}, u32[]{:S(2)}, u32[]{:S(2)}) %collective-permute-start.2) | collective-permute-done | bytes 2097184 | tf_op jit(solution)/shard_map/ppermute | solution.py:310
  104.6 8.2 %collective-permute-start.3 = (f32[2048,256]{1,0:T(8,128)}, f32[2048,256]{1,0:T(8,128)}, u32[]{:S(2)}, u32[]{:S(2)}) collective-permute-start(f32[2048,256]{1,0:T(8,128)} %get-tuple-element.43), channel_id=1, source_target_pairs={{0,2},{5,7},{10,8},{15,13},{16,18},{21,23},{26,24},{31,29}} | collective-permute-start | bytes 6291464 | tf_op jit(solution)/shard_map/ppermute | solution.py:293
  114.5 18.1 %trans.2 = f32[4096,256]{1,0:T(8,128)} custom-call(s32[10]{0:T(128)} %constant.106.clone.at, s32[10]{0:T(128)} %constant.107.clone.bt, bf16[2048,4096]{1,0:T(8,128)(2,1)} %get-tuple-element.44.h_ref, bf16[2048,4096]{1,0:T(8,128)(2,1)} %get-tuple-element.45.l_ref, f32[2048,256]{1,0:T(8,128)} %broadcast_select_fusion.11.v_ref.refs_1_), custom_call_target="tpu_custom_call" | custom-call | flops 8053063680 | bytes 20971520 | tf_op jit(solution)/shard_map/trans/pallas_call | solution.py:145
  132.6 19.0 %collective-permute-done.5 = f32[2048,256]{1,0:T(8,128)} collective-permute-done((f32[2048,256]{1,0:T(8,128)}, f32[2048,256]{1,0:T(8,128)}, u32[]{:S(2)}, u32[]{:S(2)}) %collective-permute-start.5) | collective-permute-done | bytes 2097184 | tf_op jit(solution)/shard_map/ppermute | solution.py:310
  162.4 7.3 %collective-permute-start.4 = (f32[2048,256]{1,0:T(8,128)}, f32[2048,256]{1,0:T(8,128)}, u32[]{:S(2)}, u32[]{:S(2)}) collective-permute-start(f32[2048,256]{1,0:T(8,128)} %broadcast_select_fusion.6), channel_id=1, source_target_pairs={{0,1},{2,3},{5,4},{7,6},{8,9},{10,11},{13,12},{15,14},{16,17},{18,... | collective-permute-start | bytes 6291464 | tf_op jit(solution)/shard_map/ppermute | solution.py:293
  171.6 38.8 %collective-permute-done.7 = f32[2048,256]{1,0:T(8,128)} collective-permute-done((f32[2048,256]{1,0:T(8,128)}, f32[2048,256]{1,0:T(8,128)}, u32[]{:S(2)}, u32[]{:S(2)}) %collective-permute-start.7) | collective-permute-done | bytes 2097184 | tf_op jit(solution)/shard_map/ppermute | solution.py:310
  220.8 18.1 %trans.3 = f32[4096,256]{1,0:T(8,128)} custom-call(s32[10]{0:T(128)} %constant.106.clone.at, s32[10]{0:T(128)} %constant.107.clone.bt, bf16[2048,4096]{1,0:T(8,128)(2,1)} %get-tuple-element.44.h_ref, bf16[2048,4096]{1,0:T(8,128)(2,1)} %get-tuple-element.45.l_ref, f32[2048,256]{1,0:T(8,128)} %broadcast_select_fusion.10.v_ref.refs_2_), custom_call_target="tpu_custom_call" | custom-call | flops 8053063680 | bytes 20971520 | tf_op jit(solution)/shard_map/trans/pallas_call | solution.py:145
  245.9 8.8 %collective-permute-done.13 = f32[512,256]{1,0:T(8,128)S(1)} collective-permute-done((f32[512,256]{1,0:T(8,128)S(1)}, f32[512,256]{1,0:T(8,128)S(1)}, u32[]{:S(2)}, u32[]{:S(2)}) %collective-permute-start.13) | collective-permute-done | bytes 524320 | tf_op jit(solution)/shard_map/ppermute | solution.py:336
  255.7 5.6 %collective-permute-done.11 = f32[512,256]{1,0:T(8,128)} collective-permute-done((f32[512,256]{1,0:T(8,128)S(1)}, f32[512,256]{1,0:T(8,128)}, u32[]{:S(2)}, u32[]{:S(2)}) %collective-permute-start.11) | collective-permute-done | bytes 524320 | tf_op jit(solution)/shard_map/ppermute | solution.py:336
  262.9 25.3 %collective-permute-done.15 = f32[2048,256]{1,0:T(8,128)} collective-permute-done((f32[2048,256]{1,0:T(8,128)S(1)}, f32[2048,256]{1,0:T(8,128)}, u32[]{:S(2)}, u32[]{:S(2)}) %collective-permute-start.15) | collective-permute-done | bytes 2097184 | tf_op jit(solution)/shard_map/ppermute | solution.py:310
  302.7 11.3 %collective-permute-done.17 = f32[512,256]{1,0:T(8,128)S(1)} collective-permute-done((f32[512,256]{1,0:T(8,128)S(1)}, f32[512,256]{1,0:T(8,128)S(1)}, u32[]{:S(2)}, u32[]{:S(2)}) %collective-permute-start.17) | collective-permute-done | bytes 524320 | tf_op jit(solution)/shard_map/ppermute | solution.py:336
  314.0 11.1 %collective-permute-done.19 = f32[512,256]{1,0:T(8,128)S(1)} collective-permute-done((f32[512,256]{1,0:T(8,128)S(1)}, f32[512,256]{1,0:T(8,128)S(1)}, u32[]{:S(2)}, u32[]{:S(2)}) %collective-permute-start.19) | collective-permute-done | bytes 524320 | tf_op jit(solution)/shard_map/ppermute | solution.py:336
  331.8 9.7 %collective-permute-done.22 = f32[512,256]{1,0:T(8,128)S(1)} collective-permute-done((f32[512,256]{1,0:T(8,128)S(1)}, f32[512,256]{1,0:T(8,128)S(1)}, u32[]{:S(2)}, u32[]{:S(2)}) %collective-permute-start.22) | collective-permute-done | bytes 524320 | tf_op jit(solution)/shard_map/ppermute | solution.py:336
  341.5 8.1 %collective-permute-done.21 = f32[512,256]{1,0:T(8,128)S(1)} collective-permute-done((f32[512,256]{1,0:T(8,128)S(1)}, f32[512,256]{1,0:T(8,128)S(1)}, u32[]{:S(2)}, u32[]{:S(2)}) %collective-permute-start.21) | collective-permute-done | bytes 524320 | tf_op jit(solution)/shard_map/ppermute | solution.py:336
  369.3 34.0 %near.1.x_ref = f32[2048,4096]{1,0:T(8,128)} custom-call(s32[10]{0:T(128)} %constant.106.clone.at, s32[10]{0:T(128)} %constant.107.clone.bt, f32[2048,32,128]{2,1,0:T(8,128)} %bitcast.54, f32[2048,256]{1,0:T(8,128)} %broadcast_select_fusion.11.v_ref.refs_1_, f32[2048,256]{1,0:T(8,128)} %broadcast_select_fusion.10.v_ref.refs_2_, f32[4096,256]{1,0:T(8,128)} %copy-done.2, ...), custom_call_target="tpu_custom_call" | custom-call | flops 16106127360 | bytes 20971520 | tf_op jit(solution)/shard_map/near/pallas_call | solution.py:188
  403.4 4.5 collective-permute-start.27
  414.0 8.6 %collective-permute-start.29 = (f32[64,512]{1,0:T(8,128)S(1)}, f32[64,512]{1,0:T(8,128)S(1)}, u32[]{:S(2)}, u32[]{:S(2)}) collective-permute-start(f32[64,512]{1,0:T(8,128)S(1)} %add.117), channel_id=1, source_target_pairs={{0,4},{4,0},{8,12},{12,8},{16,20},{20,16},{24,28},{28,24},{1,5},{5... | collective-permute-start | bytes 393224 | tf_op jit(solution)/shard_map/ppermute | solution.py:313
  422.7 5.0 collective-permute-start.25
  438.1 11.5 %collective-permute-done.31 = f32[256,512]{1,0:T(8,128)S(1)} collective-permute-done((f32[256,512]{1,0:T(8,128)}, f32[256,512]{1,0:T(8,128)S(1)}, u32[]{:S(2)}, u32[]{:S(2)}) %collective-permute-start.31) | collective-permute-done | bytes 524320 | tf_op jit(solution)/shard_map/ppermute | solution.py:313
  455.1 17.5 %collective-permute-done.32 = f32[2048,256]{1,0:T(8,128)} collective-permute-done((f32[2048,256]{1,0:T(8,128)}, f32[2048,256]{1,0:T(8,128)}, u32[]{:S(2)}, u32[]{:S(2)}) %collective-permute-start.32) | collective-permute-done | bytes 2097184 | tf_op jit(solution)/shard_map/ppermute | solution.py:293
  477.4 44.2 %far.1 = f32[2048,32,128]{2,1,0:T(8,128)} custom-call(s32[16]{0:T(128)} %constant.108.clone.at, s32[16]{0:T(128)} %constant.109.clone.bt, s32[2]{0:T(128)} %pad_add_fusion.place, f32[2048,4096]{1,0:T(8,128)} %near.1.x_ref, f32[2048,512]{1,0:T(8,128)} %maximum_subtract_fusion.y_ref, f32[4096,512]{1,0:T(8,128)} %bitcast.60), custom_call_target="tpu_custom_call" | custom-call | flops 16106127360 | bytes 20971520 | tf_op jit(solution)/shard_map/far/pallas_call | solution.py:233
  (124 shorter events, 114.8 us)
Async XLA Ops:
  4.6 51.1 %collective-permute-start = (f32[2048,256]{1,0:T(8,128)S(1)}, f32[2048,256]{1,0:T(8,128)}, u32[]{:S(2)}, u32[]{:S(2)}) collective-permute-start(f32[2048,256]{1,0:T(8,128)S(1)} %get-tuple-element.36), channel_id=1, source_target_pairs={{0,2},{5,7},{10,8},{15,13},{16,18},{21,23},{26,24},{31,29}} | collective-permute-start | bytes 6291464 | tf_op jit(solution)/shard_map/ppermute | solution.py:293
  54.4 45.7 %collective-permute-start.2 = (f32[2048,256]{1,0:T(8,128)}, f32[2048,256]{1,0:T(8,128)}, u32[]{:S(2)}, u32[]{:S(2)}) collective-permute-start(f32[2048,256]{1,0:T(8,128)} %get-tuple-element.40), channel_id=1, source_target_pairs={{1,0},{3,2},{4,5},{6,7},{9,8},{11,10},{12,13},{14,15},{17,16},{19,... | collective-permute-start | bytes 6291464 | tf_op jit(solution)/shard_map/ppermute | solution.py:310
  57.7 55.2 %collective-permute-start.1 = (f32[2048,256]{1,0:T(8,128)S(1)}, f32[2048,256]{1,0:T(8,128)}, u32[]{:S(2)}, u32[]{:S(2)}) collective-permute-start(f32[2048,256]{1,0:T(8,128)S(1)} %broadcast_select_fusion.7), channel_id=1, source_target_pairs={{0,1},{2,3},{5,4},{7,6},{8,9},{10,11},{13,12},{15,14},{16,17},{18,... | collective-permute-start | bytes 6291464 | tf_op jit(solution)/shard_map/ppermute | solution.py:293
  103.2 48.3 %collective-permute-start.5 = (f32[2048,256]{1,0:T(8,128)}, f32[2048,256]{1,0:T(8,128)}, u32[]{:S(2)}, u32[]{:S(2)}) collective-permute-start(f32[2048,256]{1,0:T(8,128)} %add.95), channel_id=1, source_target_pairs={{2,0},{7,5},{8,10},{13,15},{18,16},{23,21},{24,26},{29,31}} | collective-permute-start | bytes 6291464 | tf_op jit(solution)/shard_map/ppermute | solution.py:310
  104.6 54.2 %collective-permute-start.3 = (f32[2048,256]{1,0:T(8,128)}, f32[2048,256]{1,0:T(8,128)}, u32[]{:S(2)}, u32[]{:S(2)}) collective-permute-start(f32[2048,256]{1,0:T(8,128)} %get-tuple-element.43), channel_id=1, source_target_pairs={{0,2},{5,7},{10,8},{15,13},{16,18},{21,23},{26,24},{31,29}} | collective-permute-start | bytes 6291464 | tf_op jit(solution)/shard_map/ppermute | solution.py:293
  161.2 49.2 %collective-permute-start.7 = (f32[2048,256]{1,0:T(8,128)}, f32[2048,256]{1,0:T(8,128)}, u32[]{:S(2)}, u32[]{:S(2)}) collective-permute-start(f32[2048,256]{1,0:T(8,128)} %get-tuple-element.49), channel_id=1, source_target_pairs={{1,0},{3,2},{4,5},{6,7},{9,8},{11,10},{12,13},{14,15},{17,16},{19,... | collective-permute-start | bytes 6291464 | tf_op jit(solution)/shard_map/ppermute | solution.py:310
  162.4 55.1 %collective-permute-start.4 = (f32[2048,256]{1,0:T(8,128)}, f32[2048,256]{1,0:T(8,128)}, u32[]{:S(2)}, u32[]{:S(2)}) collective-permute-start(f32[2048,256]{1,0:T(8,128)} %broadcast_select_fusion.6), channel_id=1, source_target_pairs={{0,1},{2,3},{5,4},{7,6},{8,9},{10,11},{13,12},{15,14},{16,17},{18,... | collective-permute-start | bytes 6291464 | tf_op jit(solution)/shard_map/ppermute | solution.py:293
  214.1 24.8 %collective-permute-start.8 = (f32[512,256]{1,0:T(8,128)}, f32[512,256]{1,0:T(8,128)S(1)}, u32[]{:S(2)}, u32[]{:S(2)}) collective-permute-start(f32[512,256]{1,0:T(8,128)} %get-tuple-element.89), channel_id=1, source_target_pairs={{0,8},{4,12},{8,0},{12,4},{16,24},{20,28},{24,16},{28,20},{1,9},{5... | collective-permute-start | bytes 1572872 | tf_op jit(solution)/shard_map/ppermute | solution.py:336
  214.1 24.8 %collective-permute-start.10 = (f32[512,256]{1,0:T(8,128)}, f32[512,256]{1,0:T(8,128)S(1)}, u32[]{:S(2)}, u32[]{:S(2)}) collective-permute-start(f32[512,256]{1,0:T(8,128)} %get-tuple-element.90), channel_id=1, source_target_pairs={{0,24},{4,28},{8,16},{12,20},{16,8},{20,12},{24,0},{28,4},{1,25},{... | collective-permute-start | bytes 1572872 | tf_op jit(solution)/shard_map/ppermute | solution.py:336
  217.0 22.6 %collective-permute-start.9 = (f32[512,256]{1,0:T(8,128)}, f32[512,256]{1,0:T(8,128)}, u32[]{:S(2)}, u32[]{:S(2)}) collective-permute-start(f32[512,256]{1,0:T(8,128)} %get-tuple-element.91), channel_id=1, source_target_pairs={{0,16},{4,20},{8,24},{12,28},{16,0},{20,4},{24,8},{28,12},{1,17},{... | collective-permute-start | bytes 1572872 | tf_op jit(solution)/shard_map/ppermute | solution.py:336
  242.7 18.7 %collective-permute-start.11 = (f32[512,256]{1,0:T(8,128)S(1)}, f32[512,256]{1,0:T(8,128)}, u32[]{:S(2)}, u32[]{:S(2)}) collective-permute-start(f32[512,256]{1,0:T(8,128)S(1)} %add_add_fusion.1), channel_id=1, source_target_pairs={{0,24},{4,28},{8,16},{12,20},{16,8},{20,12},{24,0},{28,4},{1,25},{... | collective-permute-start | bytes 1572872 | tf_op jit(solution)/shard_map/ppermute | solution.py:336
  244.6 43.7 %collective-permute-start.15 = (f32[2048,256]{1,0:T(8,128)S(1)}, f32[2048,256]{1,0:T(8,128)}, u32[]{:S(2)}, u32[]{:S(2)}) collective-permute-start(f32[2048,256]{1,0:T(8,128)S(1)} %add.101), channel_id=1, source_target_pairs={{2,0},{7,5},{8,10},{13,15},{18,16},{23,21},{24,26},{29,31}} | collective-permute-start | bytes 6291464 | tf_op jit(solution)/shard_map/ppermute | solution.py:310
  262.9 30.7 %collective-permute-start.14 = (f32[2048,256]{1,0:T(8,128)S(1)}, f32[2048,256]{1,0:T(8,128)S(1)}, u32[]{:S(2)}, u32[]{:S(2)}) collective-permute-start(f32[2048,256]{1,0:T(8,128)S(1)} %pad_maximum_fusion.2), channel_id=1, source_target_pairs={{0,4},{4,0},{8,12},{12,8},{16,20},{20,16},{24,28},{28,24},{1,5},{5... | collective-permute-start | bytes 6291464 | tf_op jit(solution)/shard_map/ppermute | solution.py:313
  297.2 33.0 %collective-permute-start.23 = (f32[2048,256]{1,0:T(8,128)S(1)}, f32[2048,256]{1,0:T(8,128)S(1)}, u32[]{:S(2)}, u32[]{:S(2)}) collective-permute-start(f32[2048,256]{1,0:T(8,128)S(1)} %bitcast.68), channel_id=1, source_target_pairs={{0,2},{5,7},{10,8},{15,13},{16,18},{21,23},{26,24},{31,29}} | collective-permute-start | bytes 6291464 | tf_op jit(solution)/shard_map/ppermute | solution.py:293
  299.2 14.9 %collective-permute-start.17 = (f32[512,256]{1,0:T(8,128)S(1)}, f32[512,256]{1,0:T(8,128)S(1)}, u32[]{:S(2)}, u32[]{:S(2)}) collective-permute-start(f32[512,256]{1,0:T(8,128)S(1)} %get-tuple-element.81), channel_id=1, source_target_pairs={{0,8},{4,12},{8,0},{12,4},{16,24},{20,28},{24,16},{28,20},{1,9},{5... | collective-permute-start | bytes 1572872 | tf_op jit(solution)/shard_map/ppermute | solution.py:336
  299.2 25.9 %collective-permute-start.19 = (f32[512,256]{1,0:T(8,128)S(1)}, f32[512,256]{1,0:T(8,128)S(1)}, u32[]{:S(2)}, u32[]{:S(2)}) collective-permute-start(f32[512,256]{1,0:T(8,128)S(1)} %get-tuple-element.82), channel_id=1, source_target_pairs={{0,24},{4,28},{8,16},{12,20},{16,8},{20,12},{24,0},{28,4},{1,25},{... | collective-permute-start | bytes 1572872 | tf_op jit(solution)/shard_map/ppermute | solution.py:336
  302.2 24.3 %collective-permute-start.18 = (f32[512,256]{1,0:T(8,128)S(1)}, f32[512,256]{1,0:T(8,128)S(1)}, u32[]{:S(2)}, u32[]{:S(2)}) collective-permute-start(f32[512,256]{1,0:T(8,128)S(1)} %get-tuple-element.83), channel_id=1, source_target_pairs={{0,16},{4,20},{8,24},{12,28},{16,0},{20,4},{24,8},{28,12},{1,17},{... | collective-permute-start | bytes 1572872 | tf_op jit(solution)/shard_map/ppermute | solution.py:336
  326.6 14.9 %collective-permute-start.22 = (f32[512,256]{1,0:T(8,128)S(1)}, f32[512,256]{1,0:T(8,128)S(1)}, u32[]{:S(2)}, u32[]{:S(2)}) collective-permute-start(f32[512,256]{1,0:T(8,128)S(1)} %add_add_fusion), channel_id=1, source_target_pairs={{0,8},{4,12},{8,0},{12,4},{16,24},{20,28},{24,16},{28,20},{1,9},{5... | collective-permute-start | bytes 1572872 | tf_op jit(solution)/shard_map/ppermute | solution.py:336
  327.1 22.5 %collective-permute-start.21 = (f32[512,256]{1,0:T(8,128)S(1)}, f32[512,256]{1,0:T(8,128)S(1)}, u32[]{:S(2)}, u32[]{:S(2)}) collective-permute-start(f32[512,256]{1,0:T(8,128)S(1)} %add_add_fusion), channel_id=1, source_target_pairs={{0,16},{4,20},{8,24},{12,28},{16,0},{20,4},{24,8},{28,12},{1,17},{... | collective-permute-start | bytes 1572872 | tf_op jit(solution)/shard_map/ppermute | solution.py:336
  327.6 22.0 %collective-permute-start.20 = (f32[512,256]{1,0:T(8,128)S(1)}, f32[512,256]{1,0:T(8,128)S(1)}, u32[]{:S(2)}, u32[]{:S(2)}) collective-permute-start(f32[512,256]{1,0:T(8,128)S(1)} %add_add_fusion), channel_id=1, source_target_pairs={{0,24},{4,28},{8,16},{12,20},{16,8},{20,12},{24,0},{28,4},{1,25},{... | collective-permute-start | bytes 1572872 | tf_op jit(solution)/shard_map/ppermute | solution.py:336
  361.2 49.6 %collective-permute-start.28 = (f32[2048,256]{1,0:T(8,128)}, f32[2048,256]{1,0:T(8,128)}, u32[]{:S(2)}, u32[]{:S(2)}) collective-permute-start(f32[2048,256]{1,0:T(8,128)} %bitcast.29), channel_id=1, source_target_pairs={{0,2},{5,7},{10,8},{15,13},{16,18},{21,23},{26,24},{31,29}} | collective-permute-start | bytes 6291464 | tf_op jit(solution)/shard_map/ppermute | solution.py:293
  369.3 34.1 %collective-permute-start.26 = (f32[64,512]{1,0:T(8,128)S(1)}, f32[64,512]{1,0:T(8,128)S(1)}, u32[]{:S(2)}, u32[]{:S(2)}) collective-permute-start(f32[64,512]{1,0:T(8,128)S(1)} %pad_maximum_fusion.6), channel_id=1, source_target_pairs={{0,2},{1,3},{2,0},{3,1},{4,6},{5,7},{6,4},{7,5},{8,10},{9,11},{10,... | collective-permute-start | bytes 393224 | tf_op jit(solution)/shard_map/ppermute | solution.py:313
  422.7 30.5 %collective-permute-start.25 = (f32[2048,256]{1,0:T(8,128)}, f32[2048,256]{1,0:T(8,128)}, u32[]{:S(2)}, u32[]{:S(2)}) collective-permute-start(f32[2048,256]{1,0:T(8,128)} %broadcast_select_fusion.5), channel_id=1, source_target_pairs={{0,1},{2,3},{5,4},{7,6},{8,9},{10,11},{13,12},{15,14},{16,17},{18,... | collective-permute-start | bytes 6291464 | tf_op jit(solution)/shard_map/ppermute | solution.py:293
  431.7 40.9 %collective-permute-start.32 = (f32[2048,256]{1,0:T(8,128)}, f32[2048,256]{1,0:T(8,128)}, u32[]{:S(2)}, u32[]{:S(2)}) collective-permute-start(f32[2048,256]{1,0:T(8,128)} %broadcast_select_fusion.4), channel_id=1, source_target_pairs={{0,1},{2,3},{5,4},{7,6},{8,9},{10,11},{13,12},{15,14},{16,17},{18,... | collective-permute-start | bytes 6291464 | tf_op jit(solution)/shard_map/ppermute | solution.py:293
  (21 other events, 231.5 us)

commit v2 on v1

--- a/solution.py
+++ b/solution.py
@@ -63,7 +63,7 @@
         return pltpu.CompilerParams(vmem_limit_bytes=60 << 20)
 
 
-def first_kernel(plan, at, bt, place, a_ref, v_ref, o0_ref, o1_ref, h_ref, l_ref, vh, vl):
+def first_kernel(plan, at, bt, place, a_ref, v_ref, o_ref, h_ref, l_ref, vh, vl):
     g = pl.program_id(0)
     a, b = at[g], bt[g]
 
@@ -75,17 +75,34 @@
     h_ref[...], l_ref[...] = x
     s = pl.ds(pl.multiple_of(b * plan.cols, plan.cols), plan.cols)
     d = dot3(x, (vh[s, :], vl[s, :]), 1, 0)
-    w = o0_ref.shape[1]
 
     @pl.when(b == 0)
     def _():
-        o0_ref[...] = d[:, :w]
-        o1_ref[...] = d[:, w:]
+        o_ref[...] = d
 
     @pl.when(b > 0)
     def _():
-        o0_ref[...] += d[:, :w]
-        o1_ref[...] += d[:, w:]
+        o_ref[...] += d
+
+
+def direct_kernel(plan, at, bt, h_ref, l_ref, v_ref, o_ref, vh, vl):
+    g = pl.program_id(0)
+    b = bt[g]
+
+    @pl.when(g == 0)
+    def _():
+        vh[...], vl[...] = split(v_ref[...])
+
+    s = pl.ds(pl.multiple_of(b * plan.cols, plan.cols), plan.cols)
+    d = dot3((h_ref[...], l_ref[...]), (vh[s, :], vl[s, :]), 1, 0)
+
+    @pl.when(b == 0)
+    def _():
+        o_ref[...] = d
+
+    @pl.when(b > 0)
+    def _():
+        o_ref[...] += d
 
 
 def whole(x):
@@ -97,9 +114,13 @@
     return pl.CostEstimate(flops=2 * passes * area * n, bytes_accessed=4 * area, transcendentals=0)
 
 
-def direct_first(plan, a, v, place):
+def strip(x, q, n):
+    return pl.BlockSpec((x.shape[0], n), lambda g, *_: (0, q), pipeline_mode=pl.Buffered(1))
+
+
+def direct_first(plan, a, v, q, width, place):
     at, bt = plan.tables([(i, j) for i in range(plan.blocks) for j in range(i + 1)])
-    n = v.shape[1]
+    n = width
     block = pl.BlockSpec((plan.rows, plan.cols), lambda g, at, bt, p: (at[g], bt[g]))
     flat = jax.ShapeDtypeStruct((a.shape[0], a.shape[1] * a.shape[2]), BF16)
     return pl.pallas_call(
@@ -107,15 +128,35 @@
         grid_spec=pltpu.PrefetchScalarGridSpec(
             num_scalar_prefetch=3,
             grid=(at.shape[0],),
-            in_specs=[plan.a_spec(lambda g, at, bt, p: (at[g], bt[g], 0)), whole(v)],
-            out_specs=[pl.BlockSpec((plan.rows, n // 2), lambda g, at, bt, p: (at[g], 0))] * 2 + [block, block],
-            scratch_shapes=[pltpu.VMEM(v.shape, BF16)] * 2,
+            in_specs=[plan.a_spec(lambda g, at, bt, p: (at[g], bt[g], 0)), strip(v, q, n)],
+            out_specs=[pl.BlockSpec((plan.rows, n), lambda g, at, bt, p: (at[g], 0)), block, block],
+            scratch_shapes=[pltpu.VMEM((v.shape[0], n), BF16)] * 2,
         ),
-        out_shape=[jax.ShapeDtypeStruct((a.shape[0], n // 2), F32)] * 2 + [flat, flat],
+        out_shape=[jax.ShapeDtypeStruct((a.shape[0], n), F32), flat, flat],
         cost_estimate=cost(plan, n),
         compiler_params=plan.params(),
         name="direct_first",
     )(at, bt, place, a, v)
+
+
+def direct(plan, h, l, v, q, width):
+    at, bt = plan.tables([(i, j) for i in range(plan.blocks) for j in range(i + 1)])
+    n = width
+    block = pl.BlockSpec((plan.rows, plan.cols), lambda g, at, bt: (at[g], bt[g]))
+    return pl.pallas_call(
+        functools.partial(direct_kernel, plan),
+        grid_spec=pltpu.PrefetchScalarGridSpec(
+            num_scalar_prefetch=2,
+            grid=(at.shape[0],),
+            in_specs=[block, block, strip(v, q, n)],
+            out_specs=pl.BlockSpec((plan.rows, n), lambda g, at, bt: (at[g], 0)),
+            scratch_shapes=[pltpu.VMEM((v.shape[0], n), BF16)] * 2,
+        ),
+        out_shape=jax.ShapeDtypeStruct((h.shape[0], n), F32),
+        cost_estimate=cost(plan, n),
+        compiler_params=plan.params(),
+        name="direct",
+    )(at, bt, h, l, v)
 
 
 def trans_kernel(plan, at, bt, h_ref, l_ref, v_ref, o_ref, vh, vl):
@@ -322,11 +363,6 @@
     def joined(x, got, bit):
         upper = jnp.bitwise_and(row, bit) != 0
         return jnp.concatenate([jnp.where(upper, got, x), jnp.where(upper, x, got)], axis=0)
-
-    def collect(x, order):
-        for bit in reversed(order):
-            x = joined(x, swap(x, "row", row_count, bit), bit)
-        return x
 
     row_bits = [1 << n for n in range(row_count.bit_length() - 1)]
     others = row_count // 2
@@ -370,21 +406,22 @@
         return t.reshape(cols, width)
 
     ga0 = hop_out(own[0], bits[-1])
-    d0, d1, high_part, low_part = direct_first(plan, a, vc, place)
+    d0, high_part, low_part = direct_first(plan, a, vc, 0, width, place)
     b0 = hop_in(d0, bits[0])
+    d1 = direct(plan, high_part, low_part, vc, 1, width)
     x0 = mid_out(take(own[0], tie(ga0, d1), bits[-1]))
     gb0 = hop_out(x0, bits[0])
     d0 = mid_in(tie(d0, x0) + b0)
     a0 = hop_in(d0, bits[-1])
-    ga1 = hop_out(tie(own[1], d0), bits[-1])
     v0 = take(tie(x0, d0), gb0, bits[0])
+    ga1 = hop_out(tie(own[1], v0), bits[-1])
+    b1 = hop_in(tie(d1, v0), bits[0])
     t0 = trans(plan, high_part, low_part, v0)
     t0 = with_direct(t0, tie(d0, t0) + a0)
     s0 = sum_steps(t0)
     next(s0)
     x1 = mid_out(take(tie(own[1], t0), ga1, bits[-1]))
     gb1 = hop_out(x1, bits[0])
-    b1 = hop_in(tie(d1, x1), bits[0])
     e = s0.send(x1)
     d1 = mid_in(tie(d1, e) + b1)
     a1 = hop_in(d1, bits[-1])
@@ -411,14 +448,18 @@
     mine = lax.dynamic_slice_in_dim(vc, row * piece, piece, axis=1)
     m = [high(tie(mine, oy1), y, 0, 0) for y in (y0, y1)]
     m = jnp.concatenate(m, axis=1)
-    got = swap(m, "col", col_count, bits[-1])
+    zs = [lax.ppermute(m, "col", [(n, n ^ c) for n in range(col_count)]) for c in range(1, col_count)]
     x = near(plan, a, [v0, v1], [(tie(y0, m), 0), (y1, 0)])
-    m = tie(m, x) + got
-    for bit in reversed(bits[:-1]):
-        m = m + swap(m, "col", col_count, bit)
+    m = tie(m, x)
+    for g in zs:
+        m = m + g
     x1 = mid_out(take(tie(oy1, m), ga1, bits[-1]))
     gb1 = hop_out(x1, bits[0])
-    m = collect(tie(m, x1), row_bits[::-1])
+    stack = [m] + [lax.ppermute(m, "row", [(n, n ^ c) for n in range(row_count)]) for c in range(1, row_count)]
+    for bit in row_bits:
+        flip = jnp.bitwise_and(row, bit) != 0
+        stack = [jnp.where(flip, stack[n ^ bit], stack[n]) for n in range(row_count)]
+    m = jnp.concatenate(stack, axis=0)
     fix = high(jnp.concatenate([v0, v1], axis=1), m, 1, 0)
     r0 = take(tie(x0, fix), gb0, bits[0])
     r1 = take(tie(x1, r0), gb1, bits[0])

time: 526 us -> 497 us (0.945)
  the two profiles are of different devices: /device:TPU:0 before, /device:TPU:1 now
where the time goes in v2:
time: 497 us; the launch traced here: 488 us
  Pallas kernels  166 us (33%)
  waiting for transfers between devices  155 us (31%)
  starting transfers between devices  93.9 us (19%)
  other arithmetic  42.7 us (9%)
  local copies, waits for them, and re-layouts  21.7 us (4%)
  matrix products  7.51 us (2%)
    ppermute x8, waiting for transfers between devices, hop_out(): return lax.ppermute(x, both, pairs(lambda code: code & ~done == 0, bit))  81 us
    ppermute x12, waiting for transfers between devices, cross(): return lax.ppermute(x, 'row', [(n, n ^ 2 * code) for n in range(row_count)])  61.3 us
    pallas_call x1, Pallas kernels, far(): pl.pallas_call(functools.partial(far_kernel, plan), grid_spec=pltpu.Prefe...  44.2 us
    pallas_call x2, Pallas kernels, trans(): pl.pallas_call(functools.partial(trans_kernel, plan), grid_spec=pltpu.Pre...  36.2 us
    pallas_call x1, Pallas kernels, near(): pl.pallas_call(functools.partial(near_kernel, plan, len(yc)), grid_spec=p...  34.1 us
    pallas_call x1, Pallas kernels, direct_first(): pl.pallas_call(functools.partial(first_kernel, plan), grid_spec=pltpu.Pre...  33.3 us
    ppermute x4, starting transfers between devices, swap(): return lax.ppermute(x, axis, [(n, n ^ bit) for n in range(count)])  29.2 us
    ppermute x8, starting transfers between devices, hop_out(): return lax.ppermute(x, both, pairs(lambda code: code & ~done == 0, bit))  24.5 us
  transfers between devices with their start and end apart: 38, of which 16 were waited for; matrix products, arithmetic and copies ran while one was open for 9% of the time, Pallas kernels for 25%

profile of v2, /device:TPU:1, one launch (start us, length us, event | category | flops | bytes accessed | tf_op | source)
XLA Modules:
  0.0 488.0 jit_solution(2491251434362011576)
XLA Ops:
  7.2 33.3 %direct_first.1 = (f32[2048,256]{1,0:T(8,128)}, bf16[2048,4096]{1,0:T(8,128)(2,1)}, bf16[2048,4096]{1,0:T(8,128)(2,1)}) custom-call(s32[10]{0:T(128)} %constant.104.clone.at, s32[10]{0:T(128)} %constant.105.clone.bt, s32[2]{0:T(128)} %pad_add_fusion.place, f32[2048,32,128]{2,1,0:T(8,128)} %bitcast.54, f32[4096,512]{1,0:T(8,128)} %bitcast.57), custom_call_target="tpu_custom_call" | custom-call | flops 8053063680 | bytes 20971520 | tf_op jit(solution)/shard_map/direct_first/pallas_call | solution.py:126
  40.6 8.9 %collective-permute-start.2 = (f32[2048,256]{1,0:T(8,128)}, f32[2048,256]{1,0:T(8,128)}, u32[]{:S(2)}, u32[]{:S(2)}) collective-permute-start(f32[2048,256]{1,0:T(8,128)} %get-tuple-element.39), channel_id=1, source_target_pairs={{1,0},{3,2},{4,5},{6,7},{9,8},{11,10},{12,13},{14,15},{17,16},{19,... | collective-permute-start | bytes 6291464 | tf_op jit(solution)/shard_map/ppermute | solution.py:351
  49.4 18.3 %direct.1 = f32[2048,256]{1,0:T(8,128)} custom-call(s32[10]{0:T(128)} %constant.104.clone.at, s32[10]{0:T(128)} %constant.105.clone.bt, bf16[2048,4096]{1,0:T(8,128)(2,1)} %get-tuple-element.35.h_ref, bf16[2048,4096]{1,0:T(8,128)(2,1)} %get-tuple-element.36.l_ref, f32[4096,512]{1,0:T(8,128)} %bitcast.58), custom_call_target="tpu_custom_call" | custom-call | flops 8053063680 | bytes 20971520 | tf_op jit(solution)/shard_map/direct/pallas_call | solution.py:146
  76.6 32.2 %collective-permute-done.1 = f32[2048,256]{1,0:T(8,128)} collective-permute-done((f32[2048,256]{1,0:T(8,128)}, f32[2048,256]{1,0:T(8,128)}, u32[]{:S(2)}, u32[]{:S(2)}) %collective-permute-start.1) | collective-permute-done | bytes 2097184 | tf_op jit(solution)/shard_map/ppermute | solution.py:334
  117.4 18.1 %trans.2 = f32[4096,256]{1,0:T(8,128)} custom-call(s32[10]{0:T(128)} %constant.106.clone.at, s32[10]{0:T(128)} %constant.107.clone.bt, bf16[2048,4096]{1,0:T(8,128)(2,1)} %get-tuple-element.35.h_ref, bf16[2048,4096]{1,0:T(8,128)(2,1)} %get-tuple-element.36.l_ref, f32[2048,256]{1,0:T(8,128)} %broadcast_select_fusion.11.v_ref.refs_1_), custom_call_target="tpu_custom_call" | custom-call | flops 8053063680 | bytes 20971520 | tf_op jit(solution)/shard_map/trans/pallas_call | solution.py:186
  146.6 13.6 %collective-permute-start.4 = (f32[2048,256]{1,0:T(8,128)}, f32[2048,256]{1,0:T(8,128)}, u32[]{:S(2)}, u32[]{:S(2)}) collective-permute-start(f32[2048,256]{1,0:T(8,128)} %broadcast_select_fusion.6), channel_id=1, source_target_pairs={{0,1},{2,3},{5,4},{7,6},{8,9},{10,11},{13,12},{15,14},{16,17},{18,... | collective-permute-start | bytes 6291464 | tf_op jit(solution)/shard_map/ppermute | solution.py:334
  169.8 13.8 %collective-permute-done.4 = f32[2048,256]{1,0:T(8,128)} collective-permute-done((f32[2048,256]{1,0:T(8,128)}, f32[2048,256]{1,0:T(8,128)}, u32[]{:S(2)}, u32[]{:S(2)}) %collective-permute-start.4) | collective-permute-done | bytes 2097184 | tf_op jit(solution)/shard_map/ppermute | solution.py:334
  186.7 18.1 %trans.3 = f32[4096,256]{1,0:T(8,128)} custom-call(s32[10]{0:T(128)} %constant.106.clone.at, s32[10]{0:T(128)} %constant.107.clone.bt, bf16[2048,4096]{1,0:T(8,128)(2,1)} %get-tuple-element.35.h_ref, bf16[2048,4096]{1,0:T(8,128)(2,1)} %get-tuple-element.36.l_ref, f32[2048,256]{1,0:T(8,128)} %broadcast_select_fusion.10.v_ref.refs_2_), custom_call_target="tpu_custom_call" | custom-call | flops 8053063680 | bytes 20971520 | tf_op jit(solution)/shard_map/trans/pallas_call | solution.py:186
  211.7 9.2 %collective-permute-done.13 = f32[512,256]{1,0:T(8,128)S(1)} collective-permute-done((f32[512,256]{1,0:T(8,128)S(1)}, f32[512,256]{1,0:T(8,128)S(1)}, u32[]{:S(2)}, u32[]{:S(2)}) %collective-permute-start.13) | collective-permute-done | bytes 524320 | tf_op jit(solution)/shard_map/ppermute | solution.py:372
  221.0 12.2 %collective-permute-done.11 = f32[512,256]{1,0:T(8,128)} collective-permute-done((f32[512,256]{1,0:T(8,128)S(1)}, f32[512,256]{1,0:T(8,128)}, u32[]{:S(2)}, u32[]{:S(2)}) %collective-permute-start.11) | collective-permute-done | bytes 524320 | tf_op jit(solution)/shard_map/ppermute | solution.py:372
  240.5 24.5 %collective-permute-start.16 = (f32[2048,256]{1,0:T(8,128)S(1)}, f32[2048,256]{1,0:T(8,128)S(1)}, u32[]{:S(2)}, u32[]{:S(2)}) collective-permute-start(f32[2048,256]{1,0:T(8,128)S(1)} %get-tuple-element.75), channel_id=1, source_target_pairs={{0,4},{4,0},{8,12},{12,8},{16,20},{20,16},{24,28},{28,24},{1,5},{5... | collective-permute-start | bytes 6291464 | tf_op jit(solution)/shard_map/ppermute | solution.py:354
  272.7 10.1 %collective-permute-done.17 = f32[512,256]{1,0:T(8,128)S(1)} collective-permute-done((f32[512,256]{1,0:T(8,128)S(1)}, f32[512,256]{1,0:T(8,128)S(1)}, u32[]{:S(2)}, u32[]{:S(2)}) %collective-permute-start.17) | collective-permute-done | bytes 524320 | tf_op jit(solution)/shard_map/ppermute | solution.py:372
  282.8 12.2 %collective-permute-done.19 = f32[512,256]{1,0:T(8,128)S(1)} collective-permute-done((f32[512,256]{1,0:T(8,128)S(1)}, f32[512,256]{1,0:T(8,128)S(1)}, u32[]{:S(2)}, u32[]{:S(2)}) %collective-permute-start.19) | collective-permute-done | bytes 524320 | tf_op jit(solution)/shard_map/ppermute | solution.py:372
  299.5 6.2 %collective-permute-done.22 = f32[512,256]{1,0:T(8,128)S(1)} collective-permute-done((f32[512,256]{1,0:T(8,128)S(1)}, f32[512,256]{1,0:T(8,128)S(1)}, u32[]{:S(2)}, u32[]{:S(2)}) %collective-permute-start.22) | collective-permute-done | bytes 524320 | tf_op jit(solution)/shard_map/ppermute | solution.py:372
  306.2 10.7 %collective-permute-done.20 = f32[512,256]{1,0:T(8,128)S(1)} collective-permute-done((f32[512,256]{1,0:T(8,128)S(1)}, f32[512,256]{1,0:T(8,128)S(1)}, u32[]{:S(2)}, u32[]{:S(2)}) %collective-permute-start.20) | collective-permute-done | bytes 524320 | tf_op jit(solution)/shard_map/ppermute | solution.py:372
  318.6 4.1 collective-permute-start.24
  336.5 4.5 collective-permute-start.28
  343.4 34.1 %near.1.x_ref = f32[2048,4096]{1,0:T(8,128)} custom-call(s32[10]{0:T(128)} %constant.106.clone.at, s32[10]{0:T(128)} %constant.107.clone.bt, f32[2048,32,128]{2,1,0:T(8,128)} %bitcast.55, f32[2048,256]{1,0:T(8,128)} %broadcast_select_fusion.11.v_ref.refs_1_, f32[2048,256]{1,0:T(8,128)} %broadcast_select_fusion.10.v_ref.refs_2_, f32[4096,256]{1,0:T(8,128)} %copy-done.2, ...), custom_call_target="tpu_custom_call" | custom-call | flops 16106127360 | bytes 20971520 | tf_op jit(solution)/shard_map/near/pallas_call | solution.py:229
  377.5 4.5 collective-permute-start.35
  387.3 3.6 collective-permute-done.33
  392.3 5.1 %collective-permute-done.31 = f32[64,512]{1,0:T(8,128)S(1)} collective-permute-done((f32[64,512]{1,0:T(8,128)S(1)}, f32[64,512]{1,0:T(8,128)S(1)}, u32[]{:S(2)}, u32[]{:S(2)}) %collective-permute-start.31) | collective-permute-done | bytes 131104 | tf_op jit(solution)/shard_map/ppermute | solution.py:458
  405.0 12.8 %collective-permute-done.25 = f32[2048,256]{1,0:T(8,128)S(1)} collective-permute-done((f32[2048,256]{1,0:T(8,128)S(1)}, f32[2048,256]{1,0:T(8,128)S(1)}, u32[]{:S(2)}, u32[]{:S(2)}) %collective-permute-start.25) | collective-permute-done | bytes 2097184 | tf_op jit(solution)/shard_map/ppermute | solution.py:334
  418.1 22.2 %collective-permute-done.37 = f32[2048,256]{1,0:T(8,128)S(1)} collective-permute-done((f32[2048,256]{1,0:T(8,128)S(1)}, f32[2048,256]{1,0:T(8,128)S(1)}, u32[]{:S(2)}, u32[]{:S(2)}) %collective-permute-start.37) | collective-permute-done | bytes 2097184 | tf_op jit(solution)/shard_map/ppermute | solution.py:334
  443.4 44.2 %far.1 = f32[2048,32,128]{2,1,0:T(8,128)} custom-call(s32[16]{0:T(128)} %constant.108.clone.at, s32[16]{0:T(128)} %constant.109.clone.bt, s32[2]{0:T(128)} %pad_add_fusion.place, f32[2048,4096]{1,0:T(8,128)} %near.1.x_ref, f32[2048,512]{1,0:T(8,128)} %maximum_subtract_fusion.y_ref, f32[4096,512]{1,0:T(8,128)} %bitcast.60), custom_call_target="tpu_custom_call" | custom-call | flops 16106127360 | bytes 20971520 | tf_op jit(solution)/shard_map/far/pallas_call | solution.py:274
  (139 shorter events, 110.3 us)
Async XLA Ops:
  4.6 63.2 %collective-permute-start = (f32[2048,256]{1,0:T(8,128)S(1)}, f32[2048,256]{1,0:T(8,128)}, u32[]{:S(2)}, u32[]{:S(2)}) collective-permute-start(f32[2048,256]{1,0:T(8,128)S(1)} %get-tuple-element.34), channel_id=1, source_target_pairs={{0,2},{5,7},{10,8},{15,13},{16,18},{21,23},{26,24},{31,29}} | collective-permute-start | bytes 6291464 | tf_op jit(solution)/shard_map/ppermute | solution.py:334
  40.6 30.8 %collective-permute-start.2 = (f32[2048,256]{1,0:T(8,128)}, f32[2048,256]{1,0:T(8,128)}, u32[]{:S(2)}, u32[]{:S(2)}) collective-permute-start(f32[2048,256]{1,0:T(8,128)} %get-tuple-element.39), channel_id=1, source_target_pairs={{1,0},{3,2},{4,5},{6,7},{9,8},{11,10},{12,13},{14,15},{17,16},{19,... | collective-permute-start | bytes 6291464 | tf_op jit(solution)/shard_map/ppermute | solution.py:351
  69.4 39.5 %collective-permute-start.1 = (f32[2048,256]{1,0:T(8,128)}, f32[2048,256]{1,0:T(8,128)}, u32[]{:S(2)}, u32[]{:S(2)}) collective-permute-start(f32[2048,256]{1,0:T(8,128)} %broadcast_select_fusion.7), channel_id=1, source_target_pairs={{0,1},{2,3},{5,4},{7,6},{8,9},{10,11},{13,12},{15,14},{16,17},{18,... | collective-permute-start | bytes 6291464 | tf_op jit(solution)/shard_map/ppermute | solution.py:334
  74.7 60.8 %collective-permute-start.5 = (f32[2048,256]{1,0:T(8,128)}, f32[2048,256]{1,0:T(8,128)}, u32[]{:S(2)}, u32[]{:S(2)}) collective-permute-start(f32[2048,256]{1,0:T(8,128)} %add.98), channel_id=1, source_target_pairs={{2,0},{7,5},{8,10},{13,15},{18,16},{23,21},{24,26},{29,31}} | collective-permute-start | bytes 6291464 | tf_op jit(solution)/shard_map/ppermute | solution.py:351
  112.1 31.3 %collective-permute-start.3 = (f32[2048,256]{1,0:T(8,128)}, f32[2048,256]{1,0:T(8,128)}, u32[]{:S(2)}, u32[]{:S(2)}) collective-permute-start(f32[2048,256]{1,0:T(8,128)} %get-tuple-element.42), channel_id=1, source_target_pairs={{0,2},{5,7},{10,8},{15,13},{16,18},{21,23},{26,24},{31,29}} | collective-permute-start | bytes 6291464 | tf_op jit(solution)/shard_map/ppermute | solution.py:334
  114.2 48.5 %collective-permute-start.7 = (f32[2048,256]{1,0:T(8,128)S(1)}, f32[2048,256]{1,0:T(8,128)}, u32[]{:S(2)}, u32[]{:S(2)}) collective-permute-start(f32[2048,256]{1,0:T(8,128)S(1)} %copy-done.9), channel_id=1, source_target_pairs={{1,0},{3,2},{4,5},{6,7},{9,8},{11,10},{12,13},{14,15},{17,16},{19,... | collective-permute-start | bytes 6291464 | tf_op jit(solution)/shard_map/ppermute | solution.py:351
  146.6 37.0 %collective-permute-start.4 = (f32[2048,256]{1,0:T(8,128)}, f32[2048,256]{1,0:T(8,128)}, u32[]{:S(2)}, u32[]{:S(2)}) collective-permute-start(f32[2048,256]{1,0:T(8,128)} %broadcast_select_fusion.6), channel_id=1, source_target_pairs={{0,1},{2,3},{5,4},{7,6},{8,9},{10,11},{13,12},{15,14},{16,17},{18,... | collective-permute-start | bytes 6291464 | tf_op jit(solution)/shard_map/ppermute | solution.py:334
  167.1 37.7 %collective-permute-start.8 = (f32[512,256]{1,0:T(8,128)}, f32[512,256]{1,0:T(8,128)S(1)}, u32[]{:S(2)}, u32[]{:S(2)}) collective-permute-start(f32[512,256]{1,0:T(8,128)} %get-tuple-element.95), channel_id=1, source_target_pairs={{0,8},{4,12},{8,0},{12,4},{16,24},{20,28},{24,16},{28,20},{1,9},{5... | collective-permute-start | bytes 1572872 | tf_op jit(solution)/shard_map/ppermute | solution.py:372
  167.1 37.7 %collective-permute-start.10 = (f32[512,256]{1,0:T(8,128)}, f32[512,256]{1,0:T(8,128)S(1)}, u32[]{:S(2)}, u32[]{:S(2)}) collective-permute-start(f32[512,256]{1,0:T(8,128)} %get-tuple-element.96), channel_id=1, source_target_pairs={{0,24},{4,28},{8,16},{12,20},{16,8},{20,12},{24,0},{28,4},{1,25},{... | collective-permute-start | bytes 1572872 | tf_op jit(solution)/shard_map/ppermute | solution.py:372
  169.6 36.1 %collective-permute-start.9 = (f32[512,256]{1,0:T(8,128)}, f32[512,256]{1,0:T(8,128)}, u32[]{:S(2)}, u32[]{:S(2)}) collective-permute-start(f32[512,256]{1,0:T(8,128)} %get-tuple-element.97), channel_id=1, source_target_pairs={{0,16},{4,20},{8,24},{12,28},{16,0},{20,4},{24,8},{28,12},{1,17},{... | collective-permute-start | bytes 1572872 | tf_op jit(solution)/shard_map/ppermute | solution.py:372
  208.4 24.8 %collective-permute-start.11 = (f32[512,256]{1,0:T(8,128)S(1)}, f32[512,256]{1,0:T(8,128)}, u32[]{:S(2)}, u32[]{:S(2)}) collective-permute-start(f32[512,256]{1,0:T(8,128)S(1)} %add_add_fusion.1), channel_id=1, source_target_pairs={{0,24},{4,28},{8,16},{12,20},{16,8},{20,12},{24,0},{28,4},{1,25},{... | collective-permute-start | bytes 1572872 | tf_op jit(solution)/shard_map/ppermute | solution.py:372
  209.7 25.6 %collective-permute-start.15 = (f32[2048,256]{1,0:T(8,128)S(1)}, f32[2048,256]{1,0:T(8,128)}, u32[]{:S(2)}, u32[]{:S(2)}) collective-permute-start(f32[2048,256]{1,0:T(8,128)S(1)} %copy-done.10), channel_id=1, source_target_pairs={{2,0},{7,5},{8,10},{13,15},{18,16},{23,21},{24,26},{29,31}} | collective-permute-start | bytes 6291464 | tf_op jit(solution)/shard_map/ppermute | solution.py:351
  234.7 30.3 %collective-permute-start.14 = (f32[2048,256]{1,0:T(8,128)S(1)}, f32[2048,256]{1,0:T(8,128)S(1)}, u32[]{:S(2)}, u32[]{:S(2)}) collective-permute-start(f32[2048,256]{1,0:T(8,128)S(1)} %pad_maximum_fusion.2), channel_id=1, source_target_pairs={{0,4},{4,0},{8,12},{12,8},{16,20},{20,16},{24,28},{28,24},{1,5},{5... | collective-permute-start | bytes 6291464 | tf_op jit(solution)/shard_map/ppermute | solution.py:354
  240.5 29.0 %collective-permute-start.16 = (f32[2048,256]{1,0:T(8,128)S(1)}, f32[2048,256]{1,0:T(8,128)S(1)}, u32[]{:S(2)}, u32[]{:S(2)}) collective-permute-start(f32[2048,256]{1,0:T(8,128)S(1)} %get-tuple-element.75), channel_id=1, source_target_pairs={{0,4},{4,0},{8,12},{12,8},{16,20},{20,16},{24,28},{28,24},{1,5},{5... | collective-permute-start | bytes 6291464 | tf_op jit(solution)/shard_map/ppermute | solution.py:354
  268.7 29.2 %collective-permute-start.23 = (f32[2048,256]{1,0:T(8,128)S(1)}, f32[2048,256]{1,0:T(8,128)S(1)}, u32[]{:S(2)}, u32[]{:S(2)}) collective-permute-start(f32[2048,256]{1,0:T(8,128)S(1)} %bitcast.70), channel_id=1, source_target_pairs={{0,2},{5,7},{10,8},{15,13},{16,18},{21,23},{26,24},{31,29}} | collective-permute-start | bytes 6291464 | tf_op jit(solution)/shard_map/ppermute | solution.py:334
  270.0 25.0 %collective-permute-start.19 = (f32[512,256]{1,0:T(8,128)S(1)}, f32[512,256]{1,0:T(8,128)S(1)}, u32[]{:S(2)}, u32[]{:S(2)}) collective-permute-start(f32[512,256]{1,0:T(8,128)S(1)} %get-tuple-element.88), channel_id=1, source_target_pairs={{0,24},{4,28},{8,16},{12,20},{16,8},{20,12},{24,0},{28,4},{1,25},{... | collective-permute-start | bytes 1572872 | tf_op jit(solution)/shard_map/ppermute | solution.py:372
  272.4 22.6 %collective-permute-start.18 = (f32[512,256]{1,0:T(8,128)S(1)}, f32[512,256]{1,0:T(8,128)S(1)}, u32[]{:S(2)}, u32[]{:S(2)}) collective-permute-start(f32[512,256]{1,0:T(8,128)S(1)} %get-tuple-element.89), channel_id=1, source_target_pairs={{0,16},{4,20},{8,24},{12,28},{16,0},{20,4},{24,8},{28,12},{1,17},{... | collective-permute-start | bytes 1572872 | tf_op jit(solution)/shard_map/ppermute | solution.py:372
  295.7 21.2 %collective-permute-start.20 = (f32[512,256]{1,0:T(8,128)S(1)}, f32[512,256]{1,0:T(8,128)S(1)}, u32[]{:S(2)}, u32[]{:S(2)}) collective-permute-start(f32[512,256]{1,0:T(8,128)S(1)} %add_add_fusion), channel_id=1, source_target_pairs={{0,24},{4,28},{8,16},{12,20},{16,8},{20,12},{24,0},{28,4},{1,25},{... | collective-permute-start | bytes 1572872 | tf_op jit(solution)/shard_map/ppermute | solution.py:372
  336.5 41.0 %collective-permute-start.28 = (f32[64,512]{1,0:T(8,128)S(1)}, f32[64,512]{1,0:T(8,128)S(1)}, u32[]{:S(2)}, u32[]{:S(2)}) collective-permute-start(f32[64,512]{1,0:T(8,128)S(1)} %pad_maximum_fusion.4), channel_id=1, source_target_pairs={{0,3},{1,2},{2,1},{3,0},{4,7},{5,6},{6,5},{7,4},{8,11},{9,10},{10,... | collective-permute-start | bytes 393224 | tf_op jit(solution)/shard_map/ppermute | solution.py:451
  341.0 36.4 %collective-permute-start.27 = (f32[64,512]{1,0:T(8,128)S(1)}, f32[64,512]{1,0:T(8,128)S(1)}, u32[]{:S(2)}, u32[]{:S(2)}) collective-permute-start(f32[64,512]{1,0:T(8,128)S(1)} %pad_maximum_fusion.4), channel_id=1, source_target_pairs={{0,2},{1,3},{2,0},{3,1},{4,6},{5,7},{6,4},{7,5},{8,10},{9,11},{10,... | collective-permute-start | bytes 393224 | tf_op jit(solution)/shard_map/ppermute | solution.py:451
  341.0 36.4 %collective-permute-start.26 = (f32[64,512]{1,0:T(8,128)S(1)}, f32[64,512]{1,0:T(8,128)S(1)}, u32[]{:S(2)}, u32[]{:S(2)}) collective-permute-start(f32[64,512]{1,0:T(8,128)S(1)} %pad_maximum_fusion.4), channel_id=1, source_target_pairs={{0,1},{1,0},{2,3},{3,2},{4,5},{5,4},{6,7},{7,6},{8,9},{9,8},{10,11... | collective-permute-start | bytes 393224 | tf_op jit(solution)/shard_map/ppermute | solution.py:451
  341.4 56.3 %collective-permute-start.36 = (f32[2048,256]{1,0:T(8,128)}, f32[2048,256]{1,0:T(8,128)}, u32[]{:S(2)}, u32[]{:S(2)}) collective-permute-start(f32[2048,256]{1,0:T(8,128)} %bitcast.29), channel_id=1, source_target_pairs={{0,2},{5,7},{10,8},{15,13},{16,18},{21,23},{26,24},{31,29}} | collective-permute-start | bytes 6291464 | tf_op jit(solution)/shard_map/ppermute | solution.py:334
  391.0 26.8 %collective-permute-start.25 = (f32[2048,256]{1,0:T(8,128)S(1)}, f32[2048,256]{1,0:T(8,128)S(1)}, u32[]{:S(2)}, u32[]{:S(2)}) collective-permute-start(f32[2048,256]{1,0:T(8,128)S(1)} %copy-done.8), channel_id=1, source_target_pairs={{0,1},{2,3},{5,4},{7,6},{8,9},{10,11},{13,12},{15,14},{16,17},{18,... | collective-permute-start | bytes 6291464 | tf_op jit(solution)/shard_map/ppermute | solution.py:334
  399.7 40.6 %collective-permute-start.37 = (f32[2048,256]{1,0:T(8,128)S(1)}, f32[2048,256]{1,0:T(8,128)S(1)}, u32[]{:S(2)}, u32[]{:S(2)}) collective-permute-start(f32[2048,256]{1,0:T(8,128)S(1)} %broadcast_select_fusion.4), channel_id=1, source_target_pairs={{0,1},{2,3},{5,4},{7,6},{8,9},{10,11},{13,12},{15,14},{16,17},{18,... | collective-permute-start | bytes 6291464 | tf_op jit(solution)/shard_map/ppermute | solution.py:334
  (27 other events, 264.5 us)
